TPU v7x, 32 devices: a whole 2x2x4 slice. The times are simulated.
32 devices in a mesh: batch: 2 (over y), row: 4 (over x, core), col: 4 (over z).
Axes of the slice: x: 2, y: 2, z: 4, core: 2. Of those that a mesh axis runs over, the one named last changes fastest.
Arguments:
- patches: bfloat16 [2, 4096, 1280], P('batch', 'col', 'row'), may hold values from -6 to 6
- qkv_weight: bfloat16 [1280, 3, 1280], P('row', None, 'col'), may hold values from -0.15625 to 0.15625
- qv_bias: float32 [2, 1280], P(None, 'col'), may hold values from -0.6 to 0.6
- proj_weight: bfloat16 [1280, 1280], P('col', 'row'), may hold values from -2.5 to 2.5
- proj_bias: float32 [1280], P('row'), may hold values from -1.2 to 1.2
- norm1_gain: float32 [1280], P('row'), may hold values from 0.5 to 1.5
- norm1_shift: float32 [1280], P('row'), may hold values from -1.2 to 1.2
- norm2_gain: float32 [1280], P('row'), may hold values from 0.5 to 1.5
- norm2_shift: float32 [1280], P('row'), may hold values from -1.2 to 1.2
- fc1_weight: bfloat16 [1280, 5120], P('row', 'col'), may hold values from -0.15625 to 0.15625
- fc1_bias: float32 [5120], P('col'), may hold values from -1.2 to 1.2
- fc2_weight: bfloat16 [5120, 1280], P('col', 'row'), may hold values from -0.078125 to 0.078125
- fc2_bias: float32 [1280], P('row'), may hold values from -1.2 to 1.2
- height_table: bfloat16 [127, 80], replicated, may hold values from -0.625 to 0.625
- width_table: bfloat16 [127, 80], replicated, may hold values from -0.625 to 0.625
- out_grad: bfloat16 [2, 4096, 1280], P('batch', 'col', 'row'), may hold values from -6 to 6
Outputs:
- block_out: bfloat16 [2, 4096, 1280], P('batch', 'col', 'row')
- patches_grad: float32 [2, 4096, 1280], P('batch', 'col', 'row')
- qkv_weight_grad: float32 [1280, 3, 1280], P('row', None, 'col')
- qv_bias_grad: float32 [2, 1280], P(None, 'col')
- proj_weight_grad: float32 [1280, 1280], P('col', 'row')
- proj_bias_grad: float32 [1280], P('row')
- norm1_gain_grad: float32 [1280], P('row')
- norm1_shift_grad: float32 [1280], P('row')
- norm2_gain_grad: float32 [1280], P('row')
- norm2_shift_grad: float32 [1280], P('row')
- fc1_weight_grad: float32 [1280, 5120], P('row', 'col')
- fc1_bias_grad: float32 [5120], P('col')
- fc2_weight_grad: float32 [5120, 1280], P('col', 'row')
- fc2_bias_grad: float32 [1280], P('row')
- height_table_grad: float32 [127, 80], replicated
- width_table_grad: float32 [127, 80], replicated
All inputs are finite; a program needn't handle non-finite values.
Results may differ from a plain program's by a relative error of at most 0.012.
Values may be sent and summed in bfloat16 or wider, within the bound.
A program may use at most 256 MiB of HBM per device.

v0:
```python
from functools import partial
import jax
import jax.numpy as jnp
from jax import lax
from jax.sharding import PartitionSpec as P

D = 1280
HEAD_DIM = 80
GRID = 64
EPSILON = 1e-06
HIGHEST = lax.Precision.HIGHEST


def feature_sums(first, second):
    return lax.psum((first, second), "row")


def rows_over_col(values):
    return lax.all_gather(values, "col", axis=0, tiled=True)


def rows_over_row(values):
    return lax.all_gather(values, "row", axis=0, tiled=True)


def sum_over_row(values):
    return lax.psum_scatter(values, "row", scatter_dimension=0, tiled=True)


def sum_over_col(values):
    return lax.psum_scatter(values, "col", scatter_dimension=0, tiled=True)


def gather_key_value(key_local, value_local):
    couple = jnp.stack([key_local, value_local], 1).astype(jnp.bfloat16)
    couple_full = lax.all_gather(couple, "row", axis=0, tiled=True)
    return (couple_full[:, 0], couple_full[:, 1])


def normalize(values, norm_gain, norm_shift, model_width):
    first, second = feature_sums(jnp.sum(values, -1), jnp.sum(values * values, -1))
    center = first / model_width
    inv_scale = lax.rsqrt(second / model_width - center * center + EPSILON)
    scaled = (values - center[:, None]) * inv_scale[:, None]
    return (scaled, inv_scale, (scaled * norm_gain + norm_shift).astype(jnp.bfloat16))


def normalize_back(grad_in, scaled, inv_scale, norm_gain, model_width):
    scaled_grad = grad_in * norm_gain
    first, second = feature_sums(jnp.sum(scaled_grad, -1), jnp.sum(scaled_grad * scaled, -1))
    return inv_scale[:, None] * (
        scaled_grad - first[:, None] / model_width - scaled * (second[:, None] / model_width)
    )


def select_table(row_count, col_count, offset, grid_side):
    shape = (row_count, col_count, 2 * grid_side - 1)
    first = lax.broadcasted_iota(jnp.int32, shape, 0) + offset
    second = lax.broadcasted_iota(jnp.int32, shape, 1)
    third = lax.broadcasted_iota(jnp.int32, shape, 2)
    return (first - second + grid_side - 1 == third).astype(jnp.bfloat16)


def head_scores(query_one, key_one, row_select, col_select, score_scale, grid_side):
    query_lines = query_one.shape[0] // grid_side
    query_grid = query_one.reshape(query_lines, grid_side, query_one.shape[1])
    rel_rows = jnp.einsum(
        "hwc,hkc->hwk", query_grid, row_select, preferred_element_type=jnp.float32
    )
    rel_cols = jnp.einsum(
        "hwc,wkc->hwk", query_grid, col_select, preferred_element_type=jnp.float32
    )
    position = (rel_rows[:, :, :, None] + rel_cols[:, :, None, :]).reshape(
        query_one.shape[0], grid_side * grid_side
    )
    raw = jnp.einsum("qc,kc->qk", query_one, key_one, preferred_element_type=jnp.float32)
    return raw * score_scale + position


def shards(
    patches,
    qkv_weight,
    qv_bias,
    proj_weight,
    proj_bias,
    norm1_gain,
    norm1_shift,
    norm2_gain,
    norm2_shift,
    fc1_weight,
    fc1_bias,
    fc2_weight,
    fc2_bias,
    height_table,
    width_table,
    out_grad,
):
    grid_side = GRID
    model_width = D
    head_size = HEAD_DIM
    score_scale = head_size ** (-0.5)
    local_cols = qkv_weight.shape[2]
    head_count = local_cols // head_size
    image_tokens = grid_side * grid_side
    query_rows = image_tokens // lax.axis_size("row")
    query_lines = query_rows // grid_side
    residual = patches[0].astype(jnp.float32)
    scaled1, inv_scale1, normed1 = normalize(residual, norm1_gain, norm1_shift, model_width)
    gathered1 = rows_over_col(normed1)
    partial_qkv = jnp.einsum(
        "lf,fkh->lkh", gathered1, qkv_weight, preferred_element_type=jnp.float32
    )
    local_qkv = sum_over_row(partial_qkv)
    queries = local_qkv[:, 0] + qv_bias[0]
    key_full, value_full = gather_key_value(local_qkv[:, 1], local_qkv[:, 2] + qv_bias[1])
    queries = queries.astype(jnp.bfloat16)
    row_onehot = select_table(
        query_lines, grid_side, lax.axis_index("row") * query_lines, grid_side
    )
    col_onehot = select_table(grid_side, grid_side, 0, grid_side)
    row_select = jnp.einsum(
        "ijd,dc->ijc", row_onehot, height_table, preferred_element_type=jnp.float32
    ).astype(jnp.bfloat16)
    col_select = jnp.einsum(
        "ijd,dc->ijc", col_onehot, width_table, preferred_element_type=jnp.float32
    ).astype(jnp.bfloat16)

    def split_heads(values):
        return values.reshape(values.shape[0], head_count, head_size).transpose(1, 0, 2)

    def join_heads(values):
        return values.transpose(1, 0, 2).reshape(values.shape[1], head_count * head_size)

    query_heads = split_heads(queries)
    key_heads = split_heads(key_full)
    value_heads = split_heads(value_full)

    def attend(operands):
        query_one, key_one, value_one = operands
        scores = head_scores(query_one, key_one, row_select, col_select, score_scale, grid_side)
        row_max = jnp.max(scores, -1, keepdims=True)
        raw_weights = jnp.exp(scores - row_max)
        row_total = jnp.sum(raw_weights, -1, keepdims=True)
        weights = (raw_weights / row_total).astype(jnp.bfloat16)
        result = jnp.dot(weights, value_one, preferred_element_type=jnp.float32).astype(
            jnp.bfloat16
        )
        return (result, (row_max + jnp.log(row_total))[:, 0])

    attended, log_total = lax.map(attend, (query_heads, key_heads, value_heads))
    merged = join_heads(attended)
    gathered_attn = rows_over_row(merged)
    projected = sum_over_col(
        jnp.dot(gathered_attn, proj_weight, preferred_element_type=jnp.float32)
    )
    middle = residual + (projected + proj_bias)
    scaled2, inv_scale2, normed2 = normalize(middle, norm2_gain, norm2_shift, model_width)
    gathered2 = rows_over_col(normed2)
    preact = (
        sum_over_row(jnp.dot(gathered2, fc1_weight, preferred_element_type=jnp.float32)) + fc1_bias
    )
    activated = jax.nn.gelu(preact, approximate=False).astype(jnp.bfloat16)
    gathered_act = rows_over_row(activated)
    lowered = sum_over_col(jnp.dot(gathered_act, fc2_weight, preferred_element_type=jnp.float32))
    final = middle + (lowered + fc2_bias)
    cotangent = out_grad[0]
    cot_all = rows_over_col(cotangent)
    fc2_grad, fc2_bias_grad = (
        jnp.einsum("lh,lf->hf", gathered_act, cot_all, preferred_element_type=jnp.float32),
        jnp.sum(cot_all, 0, dtype=jnp.float32),
    )
    act_grad = sum_over_row(
        jnp.einsum("lf,hf->lh", cot_all, fc2_weight, preferred_element_type=jnp.float32)
    )
    gelu_fn = partial(jax.nn.gelu, approximate=False)
    unused, gelu_back = jax.vjp(gelu_fn, preact)
    preact_grad = gelu_back(act_grad)[0].astype(jnp.bfloat16)
    preact_all = rows_over_row(preact_grad)
    fc1_grad, fc1_bias_grad = (
        jnp.einsum("lf,lh->fh", gathered2, preact_all, preferred_element_type=jnp.float32),
        jnp.sum(preact_all, 0, dtype=jnp.float32),
    )
    normed2_grad = sum_over_col(
        jnp.einsum("lh,fh->lf", preact_all, fc1_weight, preferred_element_type=jnp.float32)
    )
    gain2_part = jnp.sum(normed2_grad * scaled2, 0)
    shift2_part = jnp.sum(normed2_grad, 0)
    middle_grad = cotangent.astype(jnp.float32) + normalize_back(
        normed2_grad, scaled2, inv_scale2, norm2_gain, model_width
    )
    branch_grad = middle_grad.astype(jnp.bfloat16)
    branch_all = rows_over_col(branch_grad)
    proj_grad, proj_bias_grad = (
        jnp.einsum("lh,lf->hf", gathered_attn, branch_all, preferred_element_type=jnp.float32),
        jnp.sum(branch_all, 0, dtype=jnp.float32),
    )
    merged_grad = sum_over_row(
        jnp.einsum("lf,hf->lh", branch_all, proj_weight, preferred_element_type=jnp.float32)
    ).astype(jnp.bfloat16)
    merged_grad_heads = split_heads(merged_grad)

    def attend_back(operands):
        query_one, key_one, value_one, grad_one, total_one = operands
        scores = head_scores(query_one, key_one, row_select, col_select, score_scale, grid_side)
        weights = jnp.exp(scores - total_one[:, None])
        weight_grad = jnp.einsum(
            "qc,kc->qk", grad_one, value_one, preferred_element_type=jnp.float32
        )
        row_inner = jnp.sum(weights * weight_grad, -1, keepdims=True)
        score_grad = (weights * (weight_grad - row_inner)).astype(jnp.bfloat16)
        value_part = jnp.einsum(
            "qk,qc->kc", weights.astype(jnp.bfloat16), grad_one, preferred_element_type=jnp.float32
        )
        key_part = (
            jnp.einsum("qk,qc->kc", score_grad, query_one, preferred_element_type=jnp.float32)
            * score_scale
        )
        query_part = jnp.dot(score_grad, key_one, preferred_element_type=jnp.float32) * score_scale
        grid_form = score_grad.astype(jnp.float32).reshape(
            query_lines, grid_side, grid_side, grid_side
        )
        row_grad = jnp.sum(grid_form, 3)
        col_grad = jnp.sum(grid_form, 2)
        query_grid = query_one.astype(jnp.float32).reshape(query_lines, grid_side, head_size)
        from_rows = jnp.einsum(
            "hwk,hkc->hwc", row_grad, row_select.astype(jnp.float32), precision=HIGHEST
        )
        from_cols = jnp.einsum(
            "hwk,wkc->hwc", col_grad, col_select.astype(jnp.float32), precision=HIGHEST
        )
        query_part = query_part + (from_rows + from_cols).reshape(query_rows, head_size)
        row_select_grad = jnp.einsum("hwk,hwc->hkc", row_grad, query_grid, precision=HIGHEST)
        col_select_grad = jnp.einsum("hwk,hwc->wkc", col_grad, query_grid, precision=HIGHEST)
        return (query_part, key_part, value_part, row_select_grad, col_select_grad)

    query_parts, key_parts, value_parts, row_sel_grads, col_sel_grads = lax.map(
        attend_back, (query_heads, key_heads, value_heads, merged_grad_heads, log_total)
    )
    kv_grad = sum_over_row(jnp.stack([join_heads(key_parts), join_heads(value_parts)], 1)).astype(
        jnp.bfloat16
    )
    query_grad = join_heads(query_parts).astype(jnp.bfloat16)
    qkv_grad_local = jnp.concatenate([query_grad[:, None], kv_grad], 1)
    qkv_all = rows_over_row(qkv_grad_local)
    qkv_grad, qv_bias_grad = (
        jnp.einsum("lf,lkh->fkh", gathered1, qkv_all, preferred_element_type=jnp.float32),
        jnp.stack(
            [
                jnp.sum(qkv_all[:, 0], 0, dtype=jnp.float32),
                jnp.sum(qkv_all[:, 2], 0, dtype=jnp.float32),
            ],
            0,
        ),
    )
    normed1_grad = sum_over_col(
        jnp.einsum("lkh,fkh->lf", qkv_all, qkv_weight, preferred_element_type=jnp.float32)
    )
    gain1_part = jnp.sum(normed1_grad * scaled1, 0)
    shift1_part = jnp.sum(normed1_grad, 0)
    input_grad = middle_grad + normalize_back(
        normed1_grad, scaled1, inv_scale1, norm1_gain, model_width
    )
    height_part = jnp.einsum(
        "ijd,ijc->dc", row_onehot.astype(jnp.float32), jnp.sum(row_sel_grads, 0), precision=HIGHEST
    )
    width_part = jnp.einsum(
        "ijd,ijc->dc", col_onehot.astype(jnp.float32), jnp.sum(col_sel_grads, 0), precision=HIGHEST
    )
    gain1_grad, shift1_grad, gain2_grad, shift2_grad = lax.psum(
        (gain1_part, shift1_part, gain2_part, shift2_part), ("batch", "col")
    )
    height_grad, width_grad = lax.psum((height_part, width_part), ("batch", "row", "col"))
    (
        qkv_grad,
        qv_bias_grad,
        proj_grad,
        proj_bias_grad,
        fc1_grad,
        fc1_bias_grad,
        fc2_grad,
        fc2_bias_grad,
    ) = (
        lax.psum(qkv_grad.astype(jnp.bfloat16), "batch").astype(jnp.float32),
        lax.psum(qv_bias_grad.astype(jnp.bfloat16), "batch").astype(jnp.float32),
        lax.psum(proj_grad.astype(jnp.bfloat16), "batch").astype(jnp.float32),
        lax.psum(proj_bias_grad.astype(jnp.bfloat16), "batch").astype(jnp.float32),
        lax.psum(fc1_grad.astype(jnp.bfloat16), "batch").astype(jnp.float32),
        lax.psum(fc1_bias_grad.astype(jnp.bfloat16), "batch").astype(jnp.float32),
        lax.psum(fc2_grad.astype(jnp.bfloat16), "batch").astype(jnp.float32),
        lax.psum(fc2_bias_grad.astype(jnp.bfloat16), "batch").astype(jnp.float32),
    )
    return (
        final[None].astype(jnp.bfloat16),
        input_grad[None],
        qkv_grad,
        qv_bias_grad,
        proj_grad,
        proj_bias_grad,
        gain1_grad,
        shift1_grad,
        gain2_grad,
        shift2_grad,
        fc1_grad,
        fc1_bias_grad,
        fc2_grad,
        fc2_bias_grad,
        height_grad,
        width_grad,
    )


def solution(mesh):
    in_specs = (
        P("batch", "col", "row"),
        P("row", None, "col"),
        P(None, "col"),
        P("col", "row"),
        P("row"),
        P("row"),
        P("row"),
        P("row"),
        P("row"),
        P("row", "col"),
        P("col"),
        P("col", "row"),
        P("row"),
        P(),
        P(),
        P("batch", "col", "row"),
    )
    out_specs = (
        P("batch", "col", "row"),
        P("batch", "col", "row"),
        P("row", None, "col"),
        P(None, "col"),
        P("col", "row"),
        P("row"),
        P("row"),
        P("row"),
        P("row"),
        P("row"),
        P("row", "col"),
        P("col"),
        P("col", "row"),
        P("row"),
        P(),
        P(),
    )
    return jax.shard_map(shards, mesh=mesh, in_specs=in_specs, out_specs=out_specs, check_vma=False)
```

profile of v0, /device:TPU:8, one launch (start us, length us, event | category | flops | bytes accessed | tf_op | source)
XLA Modules:
  0.0 2642.6 jit_solution(13296211281150519857)
XLA Ops:
  19.7 53.3 %all-gather.11.cloned.1.call-done = bf16[4096,320]{0,1:T(8,128)(2,1)} async-done(((bf16[1024,320]{0,1:T(8,128)(2,1)}), bf16[4096,320]{0,1:T(8,128)(2,1)}) %all-gather.11.cloned.1.call-update) | async-done | bytes 2621456 | tf_op jit(solution)/shard_map/all_gather | solution.py:19
  85.4 119.9 %reduce-scatter.10.cloned.1.call-done = f32[1024,3,320]{0,2,1:T(8,128)} async-done(((f32[4096,3,320]{0,2,1:T(8,128)}), f32[1024,3,320]{0,2,1:T(8,128)}) %reduce-scatter.10.cloned.1.call-update) | async-done | bytes 3932176 | tf_op jit(solution)/shard_map/reduce_scatter | solution.py:27
  218.2 33.4 %all-gather.13.cloned.1.call-done = bf16[4096,2,320]{0,2,1:T(8,128)(2,1)} async-done(((bf16[1024,2,320]{0,2,1:T(8,128)(2,1)}), bf16[4096,2,320]{0,2,1:T(8,128)(2,1)}) %all-gather.13.cloned.1.call-update) | async-done | bytes 5242896 | tf_op jit(solution)/shard_map/all_gather | solution.py:36
  268.2 293.5 %while.30 = (s32[]{:T(128)}, bf16[4,1024,80]{1,2,0:T(8,128)(2,1)S(1)}, f32[4,1024]{1,0:T(4,128)}, bf16[4,1024,80]{2,1,0:T(8,128)(2,1)}, bf16[4,4096,80]{2,1,0:T(...) while((s32[]{:T(128)}, ...), condition=%wide.region_8.9_spmd, body=%wide.region_5.8_spmd.sunk | while | flops 1400978432 | bytes 123054200 | solution.py:150
  594.5 93.3 %reduce-scatter.12.cloned.1.call-done = f32[1024,320]{0,1:T(8,128)} async-done(((f32[4096,320]{0,1:T(8,128)}), f32[1024,320]{0,1:T(8,128)}) %reduce-scatter.12.cloned.1.call-update) | async-done | bytes 1310736 | tf_op jit(solution)/shard_map/reduce_scatter | solution.py:31
  700.1 42.7 %all-gather.27.cloned.1.call-done = bf16[1,4096,320]{1,2,0:T(8,128)(2,1)} async-done(((bf16[1,1024,320]{1,2,0:T(8,128)(2,1)}), bf16[1,4096,320]{1,2,0:T(8,128)(2,1)}) %all-gather.27.cloned.1.call-update) | async-done | bytes 2621456 | tf_op jit(solution)/shard_map/all_gather | solution.py:19
  754.6 43.9 %all-gather.17.cloned.1.call-done = bf16[4096,320]{0,1:T(8,128)(2,1)} async-done(((bf16[1024,320]{0,1:T(8,128)(2,1)}), bf16[4096,320]{0,1:T(8,128)(2,1)}) %all-gather.17.cloned.1.call-update) | async-done | bytes 2621456 | tf_op jit(solution)/shard_map/all_gather | solution.py:19
  812.8 142.1 %reduce-scatter.18.cloned.1.call-done = f32[1024,1280]{1,0:T(8,128)} async-done(((f32[4096,1280]{1,0:T(8,128)}), f32[1024,1280]{1,0:T(8,128)}) %reduce-scatter.18.cloned.1.call-update) | async-done | bytes 5242896 | tf_op jit(solution)/shard_map/reduce_scatter | solution.py:27
  954.9 155.9 %reduce-scatter.14.cloned.1.call-done = f32[1024,1280]{1,0:T(8,128)} async-done(((f32[4096,1280]{1,0:T(8,128)}), f32[1024,1280]{1,0:T(8,128)}) %reduce-scatter.14.cloned.1.call-update) | async-done | bytes 5242896 | tf_op jit(solution)/shard_map/reduce_scatter | solution.py:27
  1126.2 70.3 %all-gather.21.cloned.1.call-done = bf16[4096,1280]{1,0:T(8,128)(2,1)} async-done(((bf16[1024,1280]{1,0:T(8,128)(2,1)}), bf16[4096,1280]{1,0:T(8,128)(2,1)}) %all-gather.21.cloned.1.call-update) | async-done | bytes 10485776 | tf_op jit(solution)/shard_map/all_gather | solution.py:23
  1209.2 93.9 %reduce-scatter.20.cloned.1.call-done = f32[1024,320]{0,1:T(8,128)} async-done(((f32[4096,320]{0,1:T(8,128)}), f32[1024,320]{0,1:T(8,128)}) %reduce-scatter.20.cloned.1.call-update) | async-done | bytes 1310736 | tf_op jit(solution)/shard_map/reduce_scatter | solution.py:31
  1316.0 52.7 %all-gather.23.cloned.1.call-done = bf16[4096,320]{0,1:T(8,128)(2,1)} async-done(((bf16[1024,320]{0,1:T(8,128)(2,1)}), bf16[4096,320]{0,1:T(8,128)(2,1)}) %all-gather.23.cloned.1.call-update) | async-done | bytes 2621456 | tf_op jit(solution)/shard_map/all_gather | solution.py:19
  1374.4 52.1 %reduce-scatter.22.cloned.1.call-done = f32[1024,320]{0,1:T(8,128)} async-done(((f32[4096,320]{0,1:T(8,128)}), f32[1024,320]{0,1:T(8,128)}) %reduce-scatter.22.cloned.1.call-update) | async-done | bytes 1310736 | tf_op jit(solution)/shard_map/reduce_scatter | solution.py:27
  1429.1 574.5 %while.31 = (s32[]{:T(128)}, bf16[4,1024,80]{1,2,0:T(8,128)(2,1)}, f32[4,4096,80]{1,2,0:T(8,128)}, f32[4,4096,80]{1,2,0:T(8,128)}, f32[4,16,64,80]{3,2,1,0:T(8,1...) while((s32[]{:T(128)}, bf16[4,1024,80]{1,2,0:T(8,128)(2,1)}, ...), condition=%wide.region_27.28_spmd, body=%wide.region_23.27_spmd.sunk | while | flops 3678845952 | bytes 353068224 | solution.py:236
  1453.0 27.9 %add.336 = f32[1024,4096]{1,0:T(8,128)} reshape(f32[16,64,64,64]{3,2,1,0:T(8,128)} %broadcast_add_fusion.5) | data formatting | bytes 33554432 | tf_op jit(solution)/shard_map/while/body/eval_jaxpr/add | solution.py:73
  1596.6 27.9 %add.336 = f32[1024,4096]{1,0:T(8,128)} reshape(f32[16,64,64,64]{3,2,1,0:T(8,128)} %broadcast_add_fusion.5) | data formatting | bytes 33554432 | tf_op jit(solution)/shard_map/while/body/eval_jaxpr/add | solution.py:73
  1740.1 27.9 %add.336 = f32[1024,4096]{1,0:T(8,128)} reshape(f32[16,64,64,64]{3,2,1,0:T(8,128)} %broadcast_add_fusion.5) | data formatting | bytes 33554432 | tf_op jit(solution)/shard_map/while/body/eval_jaxpr/add | solution.py:73
  1883.5 27.9 %add.336 = f32[1024,4096]{1,0:T(8,128)} reshape(f32[16,64,64,64]{3,2,1,0:T(8,128)} %broadcast_add_fusion.5) | data formatting | bytes 33554432 | tf_op jit(solution)/shard_map/while/body/eval_jaxpr/add | solution.py:73
  2019.9 78.4 %reduce-scatter.24.cloned.1.call-done = f32[1024,2,320]{0,2,1:T(8,128)} async-done(((f32[4096,2,320]{0,2,1:T(8,128)}), f32[1024,2,320]{0,2,1:T(8,128)}) %reduce-scatter.24.cloned.1.call-update) | async-done | bytes 2621456 | tf_op jit(solution)/shard_map/reduce_scatter | solution.py:27
  2111.5 58.5 %all-gather.19.cloned.1.call-done = bf16[4096,1280]{1,0:T(8,128)(2,1)} async-done(((bf16[1024,1280]{1,0:T(8,128)(2,1)}), bf16[4096,1280]{1,0:T(8,128)(2,1)}) %all-gather.19.cloned.1.call-update) | async-done | bytes 10485776 | tf_op jit(solution)/shard_map/all_gather | solution.py:23
  2179.6 47.3 %all-gather.25.cloned.1.call-done = bf16[4096,3,320]{0,2,1:T(8,128)(2,1)} async-done(((bf16[1024,3,320]{0,2,1:T(8,128)(2,1)}), bf16[4096,3,320]{0,2,1:T(8,128)(2,1)}) %all-gather.25.cloned.1.call-update) | async-done | bytes 7864336 | tf_op jit(solution)/shard_map/all_gather | solution.py:23
  2318.5 88.2 %reduce-scatter.26.cloned.1.call-done = f32[1024,320]{0,1:T(8,128)} async-done(((f32[4096,320]{0,1:T(8,128)}), f32[1024,320]{0,1:T(8,128)}) %reduce-scatter.26.cloned.1.call-update) | async-done | bytes 1310736 | tf_op jit(solution)/shard_map/reduce_scatter | solution.py:31
  2415.5 87.7 %reduce-scatter.16.cloned.1.call-done = f32[1024,320]{0,1:T(8,128)} async-done(((f32[4096,320]{0,1:T(8,128)}), f32[1024,320]{0,1:T(8,128)}) %reduce-scatter.16.cloned.1.call-update) | async-done | bytes 1310736 | tf_op jit(solution)/shard_map/reduce_scatter | solution.py:31
  2526.7 106.0 %all-reduce.11.cloned.1.call-done = (f32[127,80]{0,1:T(8,128)}, f32[127,80]{0,1:T(8,128)}) async-done(((f32[127,80]{0,1:T(8,128)}, f32[127,80]{0,1:T(8,128)}), (f32[127,80]{0,1:T(8,128)}, f32[127,80]{0,1:T(8,128)})) %all-reduce.11.cloned.1.call-update) | async-done | bytes 81296 | tf_op jit(solution)/shard_map/psum | solution.py:272
  (346 shorter events, 1095.4 us)
Async XLA Ops:
  7.2 791.3 %copy-start = (bf16[320,1280]{1,0:T(8,128)(2,1)S(1)}, bf16[320,1280]{1,0:T(8,128)(2,1)}, u32[]{:S(2)}) copy-start(bf16[320,1280]{1,0:T(8,128)(2,1)} %param.29) | copy-start | bytes 2457604
  7.2 65.8 %all-gather.11.cloned.1.call-start = ((), (), s32[]{:S(2)}) async-start(), calls=%async_computation.9 | async-start | bytes 3276800 | tf_op jit(solution)/shard_map/all_gather | solution.py:19
  19.7 185.7 %reduce-scatter.10.cloned.1.call-start = ((), (), s32[]{:S(2)}) async-start(), calls=%async_computation.10 | async-start | bytes 19660800 | tf_op jit(solution)/shard_map/reduce_scatter | solution.py:27
  84.7 166.8 %all-gather.13.cloned.1.call-start = ((), (), s32[]{:S(2)}) async-start(), calls=%async_computation.11 | async-start | bytes 6553600 | tf_op jit(solution)/shard_map/all_gather | solution.py:36
  211.0 377.3 %all-gather.15.cloned.1.call-start = ((), (), s32[]{:S(2)}) async-start(), calls=%async_computation.12 | async-start | bytes 3276800 | tf_op jit(solution)/shard_map/all_gather | solution.py:23
  268.2 320.1 %copy-start.13 = (bf16[320,320]{1,0:T(8,128)(2,1)S(1)}, bf16[320,320]{1,0:T(8,128)(2,1)}, u32[]{:S(2)}) copy-start(bf16[320,320]{1,0:T(8,128)(2,1)} %param.23) | copy-start | bytes 614404
  562.6 125.3 %reduce-scatter.12.cloned.1.call-start = ((), (), s32[]{:S(2)}) async-start(), calls=%async_computation.13 | async-start | bytes 6553600 | tf_op jit(solution)/shard_map/reduce_scatter | solution.py:31
  593.9 148.9 %all-gather.27.cloned.1.call-start = ((), (), s32[]{:S(2)}) async-start(), calls=%async_computation.26 | async-start | bytes 3276800 | tf_op jit(solution)/shard_map/all_gather | solution.py:19
  594.5 204.0 %all-gather.17.cloned.1.call-start = ((), (), s32[]{:S(2)}) async-start(), calls=%async_computation.14 | async-start | bytes 3276800 | tf_op jit(solution)/shard_map/all_gather | solution.py:19
  697.5 615.4 %copy-start.19 = (f32[1024]{0:T(1024)}, f32[1024]{0:T(1024)S(1)}, u32[]{:S(2)}) copy-start(f32[1024]{0:T(1024)S(1)} %get-tuple-element.230) | copy-start | bytes 12292
  697.5 615.4 %copy-start.21 = (f32[1024]{0:T(1024)}, f32[1024]{0:T(1024)S(1)}, u32[]{:S(2)}) copy-start(f32[1024]{0:T(1024)S(1)} %get-tuple-element.231) | copy-start | bytes 12292
  700.0 254.9 %reduce-scatter.18.cloned.1.call-start = ((), (), s32[]{:S(2)}) async-start(), calls=%async_computation.18 | async-start | bytes 26214400 | tf_op jit(solution)/shard_map/reduce_scatter | solution.py:27
  754.5 356.3 %reduce-scatter.14.cloned.1.call-start = ((), (), s32[]{:S(2)}) async-start(), calls=%async_computation.15 | async-start | bytes 26214400 | tf_op jit(solution)/shard_map/reduce_scatter | solution.py:27
  812.7 383.8 %all-gather.21.cloned.1.call-start = ((), (), s32[]{:S(2)}) async-start(), calls=%async_computation.19 | async-start | bytes 13107200 | tf_op jit(solution)/shard_map/all_gather | solution.py:23
  1126.1 176.9 %reduce-scatter.20.cloned.1.call-start = ((), (), s32[]{:S(2)}) async-start(), calls=%async_computation.20 | async-start | bytes 6553600 | tf_op jit(solution)/shard_map/reduce_scatter | solution.py:31
  1209.1 159.5 %all-gather.23.cloned.1.call-start = ((), (), s32[]{:S(2)}) async-start(), calls=%async_computation.21 | async-start | bytes 3276800 | tf_op jit(solution)/shard_map/all_gather | solution.py:19
  1315.9 110.5 %reduce-scatter.22.cloned.1.call-start = ((), (), s32[]{:S(2)}) async-start(), calls=%async_computation.22 | async-start | bytes 6553600 | tf_op jit(solution)/shard_map/reduce_scatter | solution.py:27
  1374.3 724.1 %reduce-scatter.24.cloned.1.call-start = ((), (), s32[]{:S(2)}) async-start(), calls=%async_computation.23 | async-start | bytes 13107200 | tf_op jit(solution)/shard_map/reduce_scatter | solution.py:27
  2012.9 157.2 %all-gather.19.cloned.1.call-start = ((), (), s32[]{:S(2)}) async-start(), calls=%async_computation.16 | async-start | bytes 13107200 | tf_op jit(solution)/shard_map/all_gather | solution.py:23
  2019.9 207.0 %all-gather.25.cloned.1.call-start = ((), (), s32[]{:S(2)}) async-start(), calls=%async_computation.24 | async-start | bytes 9830400 | tf_op jit(solution)/shard_map/all_gather | solution.py:23
  2101.8 208.8 %all-reduce.13.cloned.1.call-start = ((), (), s32[]{:S(2)}) async-start(), calls=%async_computation.28 | async-start | bytes 5242880 | tf_op jit(solution)/shard_map/psum | solution.py:283
  2235.4 171.2 %reduce-scatter.26.cloned.1.call-start = ((), (), s32[]{:S(2)}) async-start(), calls=%async_computation.25 | async-start | bytes 6553600 | tf_op jit(solution)/shard_map/reduce_scatter | solution.py:31
  2243.4 259.8 %reduce-scatter.16.cloned.1.call-start = ((), (), s32[]{:S(2)}) async-start(), calls=%async_computation.17 | async-start | bytes 6553600 | tf_op jit(solution)/shard_map/reduce_scatter | solution.py:31
  2257.3 375.4 %all-reduce.11.cloned.1.call-start = ((), (), s32[]{:S(2)}) async-start(), calls=%async_computation.27 | async-start | bytes 163840 | tf_op jit(solution)/shard_map/psum | solution.py:272
  (48 other events, 4553.0 us)
Sparse Core Ops, SparseCore 0:
  19.8 53.1 all-gather.10
  84.8 120.4 reduce-scatter.9
  211.1 40.4 all-gather.12
  562.7 25.5 all-gather.14
  594.0 93.7 reduce-scatter.11
  689.2 53.4 all-gather.26
  744.9 53.5 all-gather.16
  801.1 153.7 reduce-scatter.17
  957.7 153.1 reduce-scatter.13
  1126.3 70.1 all-gather.20
  1209.3 93.7 reduce-scatter.19
  1316.1 52.5 all-gather.22
  1374.4 51.9 reduce-scatter.21
  2013.0 85.3 reduce-scatter.23
  2099.8 70.1 all-gather.18
  2171.6 55.3 all-gather.24
  2235.5 75.0 all-reduce.12
  2312.8 93.8 reduce-scatter.25
  2408.9 94.2 reduce-scatter.15
  2509.3 123.4 all-reduce.10
where the time goes:
time: 2660 us; the launch traced here: 2640 us
  waiting for transfers between devices  1470 us (55%)
  matrix products  398 us (15%)
  local copies, waits for them, and re-layouts  380 us (14%)
  other arithmetic  324 us (12%)
  blocking collectives  52.3 us (2%)
    reduce_scatter x5, waiting for transfers between devices, sum_over_row(): return lax.psum_scatter(values, 'row', scatter_dimension=0, tiled=True)  548 us
    reduce_scatter x4, waiting for transfers between devices, sum_over_col(): return lax.psum_scatter(values, 'col', scatter_dimension=0, tiled=True)  363 us
    add x8, local copies, waits for them, and re-layouts, head_scores(): rel_rows[:, :, :, None] + rel_cols[:, :, None, :]  223 us
    all_gather x4, waiting for transfers between devices, rows_over_row(): return lax.all_gather(values, 'row', axis=0, tiled=True)  202 us
    all_gather x4, waiting for transfers between devices, rows_over_col(): return lax.all_gather(values, 'col', axis=0, tiled=True)  193 us
    dot_general x8, matrix products, head_scores(): jnp.einsum('qc,kc->qk', query_one, key_one, preferred_element_type=jnp.fl...  124 us
    psum x1, waiting for transfers between devices, shards(): lax.psum((height_part, width_part), ('batch', 'row', 'col'))  106 us
    reshape x4, local copies, waits for them, and re-layouts, attend_back(): score_grad.astype(jnp.float32)  96.1 us
  transfers between devices with their start and end apart: 20, of which 20 were waited for; matrix products, arithmetic and copies ran while one was open for 5% of the time, Pallas kernels for 0%

commit v1 on v0

--- a/solution.py
+++ b/solution.py
@@ -11,12 +11,31 @@
 HIGHEST = lax.Precision.HIGHEST
 
 
+def finish_the_axis_part(x_in):
+    comm_axis = "col"
+    shares = lax.psum(1, axis_name=comm_axis)
+    windows = []
+    for kk in tuple(range(shares)):
+        windows.append((kk, (kk + 1) % shares))
+    history = []
+    for kk in [*range(shares)]:
+        history.append((kk, (kk - 1) % shares))
+    arr_now, upper = ([x_in], [x_in])
+    for _ in range(shares // 2):
+        arr_now.append(lax.ppermute(arr_now[-1], axis_name=comm_axis, perm=windows))
+    for _ in [*range((shares - 1) // 2)]:
+        upper.append(lax.ppermute(upper[-1], axis_name=comm_axis, perm=history))
+    opened = jnp.concatenate([*arr_now[::-1], *upper[1:]], axis=0)
+    x_now = jnp.roll(opened, (lax.axis_index(comm_axis) - shares // 2) * x_in.shape[0], axis=0)
+    return x_now
+
+
 def feature_sums(first, second):
     return lax.psum((first, second), "row")
 
 
 def rows_over_col(values):
-    return lax.all_gather(values, "col", axis=0, tiled=True)
+    return finish_the_axis_part(values)
 
 
 def rows_over_row(values):

time: 2660 us -> 2570 us (0.966)
  waiting for transfers between devices: 1470 us -> 1350 us
    ppermute x0 -> x12, waiting for transfers between devices: none -> 200 us  [the longest x8 169 us: finish_the_axis_part(): arr_now.append(lax.ppermute(arr_now[-1], axis_name=comm_axis, perm=windows))]
    all_gather x4 -> x0, waiting for transfers between devices: 193 us -> none  [rows_over_col(): return lax.all_gather(values, 'col', axis=0, tiled=True)]
    reduce_scatter x4, waiting for transfers between devices: 363 us -> 287 us  [sum_over_col(): return lax.psum_scatter(values, 'col', scatter_dimension=0, tiled=True)]
    reduce_scatter x5, waiting for transfers between devices: 548 us -> 491 us  [sum_over_row(): return lax.psum_scatter(values, 'row', scatter_dimension=0, tiled=True)]
  transfers between devices with their start and end apart: 20 -> 28, of which waited for: 20 -> 28; matrix products, arithmetic and copies ran while one was open for 5% -> 5% of each run, Pallas kernels for 0% -> 0%
where the time goes in v1:
time: 2570 us; the launch traced here: 2560 us
  waiting for transfers between devices  1350 us (53%)
  local copies, waits for them, and re-layouts  386 us (15%)
  matrix products  385 us (15%)
  other arithmetic  347 us (14%)
  blocking collectives  51.1 us (2%)
  starting transfers between devices  26.7 us (1%)
    reduce_scatter x5, waiting for transfers between devices, sum_over_row(): return lax.psum_scatter(values, 'row', scatter_dimension=0, tiled=True)  491 us
    reduce_scatter x4, waiting for transfers between devices, sum_over_col(): return lax.psum_scatter(values, 'col', scatter_dimension=0, tiled=True)  287 us
    add x8, local copies, waits for them, and re-layouts, head_scores(): rel_rows[:, :, :, None] + rel_cols[:, :, None, :]  223 us
    all_gather x4, waiting for transfers between devices, rows_over_row(): return lax.all_gather(values, 'row', axis=0, tiled=True)  202 us
    ppermute x8, waiting for transfers between devices, finish_the_axis_part(): arr_now.append(lax.ppermute(arr_now[-1], axis_name=comm_axis, perm=windows))  169 us
    dot_general x8, matrix products, head_scores(): jnp.einsum('qc,kc->qk', query_one, key_one, preferred_element_type=jnp.fl...  124 us
    psum x1, waiting for transfers between devices, shards(): lax.psum((height_part, width_part), ('batch', 'row', 'col'))  106 us
    reshape x4, local copies, waits for them, and re-layouts, attend_back(): score_grad.astype(jnp.float32)  95.9 us
  transfers between devices with their start and end apart: 28, of which 28 were waited for; matrix products, arithmetic and copies ran while one was open for 5% of the time, Pallas kernels for 0%

profile of v1, /device:TPU:8, one launch (start us, length us, event | category | flops | bytes accessed | tf_op | source)
XLA Modules:
  0.0 2556.5 jit_solution(11635811184847515371)
XLA Ops:
  76.8 120.5 %reduce-scatter.10.cloned.1.call-done = f32[1024,3,320]{0,2,1:T(8,128)} async-done(((f32[4096,3,320]{0,2,1:T(8,128)}), f32[1024,3,320]{0,2,1:T(8,128)}) %reduce-scatter.10.cloned.1.call-update) | async-done | bytes 3932176 | tf_op jit(solution)/shard_map/reduce_scatter | solution.py:46
  209.9 33.7 %all-gather.6.cloned.1.call-done = bf16[4096,2,320]{0,2,1:T(8,128)(2,1)} async-done(((bf16[1024,2,320]{0,2,1:T(8,128)(2,1)}), bf16[4096,2,320]{0,2,1:T(8,128)(2,1)}) %all-gather.6.cloned.1.call-update) | async-done | bytes 5242896 | tf_op jit(solution)/shard_map/all_gather | solution.py:55
  260.2 293.7 %while.30 = (s32[]{:T(128)}, bf16[4,1024,80]{1,2,0:T(8,128)(2,1)S(1)}, f32[4,1024]{1,0:T(4,128)}, bf16[4,1024,80]{2,1,0:T(8,128)(2,1)}, bf16[4,4096,80]{2,1,0:T(...) while((s32[]{:T(128)}, ...), condition=%wide.region_8.10_spmd, body=%wide.region_5.9_spmd.sunk | while | flops 1400978432 | bytes 123054200 | solution.py:169
  273.7 27.9 %add.352 = f32[1024,4096]{1,0:T(8,128)} reshape(f32[16,64,64,64]{3,2,1,0:T(8,128)} %broadcast_add_fusion.4) | data formatting | bytes 33554432 | tf_op jit(solution)/shard_map/while/body/eval_jaxpr/add | solution.py:92
  347.1 27.9 %add.352 = f32[1024,4096]{1,0:T(8,128)} reshape(f32[16,64,64,64]{3,2,1,0:T(8,128)} %broadcast_add_fusion.4) | data formatting | bytes 33554432 | tf_op jit(solution)/shard_map/while/body/eval_jaxpr/add | solution.py:92
  420.5 27.9 %add.352 = f32[1024,4096]{1,0:T(8,128)} reshape(f32[16,64,64,64]{3,2,1,0:T(8,128)} %broadcast_add_fusion.4) | data formatting | bytes 33554432 | tf_op jit(solution)/shard_map/while/body/eval_jaxpr/add | solution.py:92
  494.0 27.9 %add.352 = f32[1024,4096]{1,0:T(8,128)} reshape(f32[16,64,64,64]{3,2,1,0:T(8,128)} %broadcast_add_fusion.4) | data formatting | bytes 33554432 | tf_op jit(solution)/shard_map/while/body/eval_jaxpr/add | solution.py:92
  588.3 38.0 %collective-permute-done.6 = bf16[1024,320]{0,1:T(8,128)(2,1)S(1)} collective-permute-done((bf16[1024,320]{0,1:T(8,128)(2,1)S(1)}, bf16[1024,320]{0,1:T(8,128)(2,1)S(1)}, u32[]{:S(2)}, u32[]{:S(2)}) %collective-permute-start.6) | collective-permute-done | bytes 655392 | tf_op jit(solution)/shard_map/ppermute | solution.py:25
  651.4 28.7 %collective-permute-done.7 = bf16[1024,320]{0,1:T(8,128)(2,1)S(1)} collective-permute-done((bf16[1024,320]{0,1:T(8,128)(2,1)S(1)}, bf16[1024,320]{0,1:T(8,128)(2,1)S(1)}, u32[]{:S(2)}, u32[]{:S(2)}) %collective-permute-start.7) | collective-permute-done | bytes 655392 | tf_op jit(solution)/shard_map/ppermute | solution.py:25
  788.7 84.1 %reduce-scatter.18.cloned.1.call-done = f32[1024,1280]{1,0:T(8,128)} async-done(((f32[4096,1280]{1,0:T(8,128)}), f32[1024,1280]{1,0:T(8,128)}) %reduce-scatter.18.cloned.1.call-update) | async-done | bytes 5242896 | tf_op jit(solution)/shard_map/reduce_scatter | solution.py:46
  872.8 155.8 %reduce-scatter.14.cloned.1.call-done = f32[1024,1280]{1,0:T(8,128)} async-done(((f32[4096,1280]{1,0:T(8,128)}), f32[1024,1280]{1,0:T(8,128)}) %reduce-scatter.14.cloned.1.call-update) | async-done | bytes 5242896 | tf_op jit(solution)/shard_map/reduce_scatter | solution.py:46
  1043.9 70.3 %all-gather.12.cloned.1.call-done = bf16[4096,1280]{1,0:T(8,128)(2,1)} async-done(((bf16[1024,1280]{1,0:T(8,128)(2,1)}), bf16[4096,1280]{1,0:T(8,128)(2,1)}) %all-gather.12.cloned.1.call-update) | async-done | bytes 10485776 | tf_op jit(solution)/shard_map/all_gather | solution.py:42
  1126.8 93.9 %reduce-scatter.20.cloned.1.call-done = f32[1024,320]{0,1:T(8,128)} async-done(((f32[4096,320]{0,1:T(8,128)}), f32[1024,320]{0,1:T(8,128)}) %reduce-scatter.20.cloned.1.call-update) | async-done | bytes 1310736 | tf_op jit(solution)/shard_map/reduce_scatter | solution.py:50
  1290.2 52.2 %reduce-scatter.22.cloned.1.call-done = f32[1024,320]{0,1:T(8,128)} async-done(((f32[4096,320]{0,1:T(8,128)}), f32[1024,320]{0,1:T(8,128)}) %reduce-scatter.22.cloned.1.call-update) | async-done | bytes 1310736 | tf_op jit(solution)/shard_map/reduce_scatter | solution.py:46
  1345.1 574.5 %while.31 = (s32[]{:T(128)}, bf16[4,1024,80]{1,2,0:T(8,128)(2,1)}, f32[4,4096,80]{1,2,0:T(8,128)}, f32[4,4096,80]{1,2,0:T(8,128)}, f32[4,16,64,80]{3,2,1,0:T(8,1...) while((s32[]{:T(128)}, bf16[4,1024,80]{1,2,0:T(8,128)(2,1)}, ...), condition=%wide.region_27.29_spmd, body=%wide.region_23.28_spmd.sunk | while | flops 3678845952 | bytes 353068224 | solution.py:255
  1369.0 27.9 %add.359 = f32[1024,4096]{1,0:T(8,128)} reshape(f32[16,64,64,64]{3,2,1,0:T(8,128)} %broadcast_add_fusion.5) | data formatting | bytes 33554432 | tf_op jit(solution)/shard_map/while/body/eval_jaxpr/add | solution.py:92
  1512.5 27.9 %add.359 = f32[1024,4096]{1,0:T(8,128)} reshape(f32[16,64,64,64]{3,2,1,0:T(8,128)} %broadcast_add_fusion.5) | data formatting | bytes 33554432 | tf_op jit(solution)/shard_map/while/body/eval_jaxpr/add | solution.py:92
  1656.0 27.9 %add.359 = f32[1024,4096]{1,0:T(8,128)} reshape(f32[16,64,64,64]{3,2,1,0:T(8,128)} %broadcast_add_fusion.5) | data formatting | bytes 33554432 | tf_op jit(solution)/shard_map/while/body/eval_jaxpr/add | solution.py:92
  1935.8 78.4 %reduce-scatter.24.cloned.1.call-done = f32[1024,2,320]{0,2,1:T(8,128)} async-done(((f32[4096,2,320]{0,2,1:T(8,128)}), f32[1024,2,320]{0,2,1:T(8,128)}) %reduce-scatter.24.cloned.1.call-update) | async-done | bytes 2621456 | tf_op jit(solution)/shard_map/reduce_scatter | solution.py:46
  2027.3 58.7 %all-gather.10.cloned.1.call-done = bf16[4096,1280]{1,0:T(8,128)(2,1)} async-done(((bf16[1024,1280]{1,0:T(8,128)(2,1)}), bf16[4096,1280]{1,0:T(8,128)(2,1)}) %all-gather.10.cloned.1.call-update) | async-done | bytes 10485776 | tf_op jit(solution)/shard_map/all_gather | solution.py:42
  2095.6 47.3 %all-gather.14.cloned.1.call-done = bf16[4096,3,320]{0,2,1:T(8,128)(2,1)} async-done(((bf16[1024,3,320]{0,2,1:T(8,128)(2,1)}), bf16[4096,3,320]{0,2,1:T(8,128)(2,1)}) %all-gather.14.cloned.1.call-update) | async-done | bytes 7864336 | tf_op jit(solution)/shard_map/all_gather | solution.py:42
  2232.7 88.1 %reduce-scatter.26.cloned.1.call-done = f32[1024,320]{0,1:T(8,128)} async-done(((f32[4096,320]{0,1:T(8,128)}), f32[1024,320]{0,1:T(8,128)}) %reduce-scatter.26.cloned.1.call-update) | async-done | bytes 1310736 | tf_op jit(solution)/shard_map/reduce_scatter | solution.py:50
  2329.8 87.5 %reduce-scatter.16.cloned.1.call-done = f32[1024,320]{0,1:T(8,128)} async-done(((f32[4096,320]{0,1:T(8,128)}), f32[1024,320]{0,1:T(8,128)}) %reduce-scatter.16.cloned.1.call-update) | async-done | bytes 1310736 | tf_op jit(solution)/shard_map/reduce_scatter | solution.py:50
  2440.8 106.1 %all-reduce.11.cloned.1.call-done = (f32[127,80]{0,1:T(8,128)}, f32[127,80]{0,1:T(8,128)}) async-done(((f32[127,80]{0,1:T(8,128)}, f32[127,80]{0,1:T(8,128)}), (f32[127,80]{0,1:T(8,128)}, f32[127,80]{0,1:T(8,128)})) %all-reduce.11.cloned.1.call-update) | async-done | bytes 81296 | tf_op jit(solution)/shard_map/psum | solution.py:291
  (378 shorter events, 1202.1 us)
Async XLA Ops:
  7.2 190.1 %reduce-scatter.10.cloned.1.call-start = ((), (), s32[]{:S(2)}) async-start(), calls=%async_computation.9 | async-start | bytes 19660800 | tf_op jit(solution)/shard_map/reduce_scatter | solution.py:46
  18.3 27.6 %collective-permute-start = (bf16[1024,320]{0,1:T(8,128)(2,1)S(1)}, bf16[1024,320]{0,1:T(8,128)(2,1)S(1)}, u32[]{:S(2)}, u32[]{:S(2)}) collective-permute-start(bf16[1024,320]{0,1:T(8,128)(2,1)S(1)} %fusion.96), channel_id=1, source_target_pairs={{0,1},{1,2},{2,3},{3,0},{4,5},{5,6},{6,7},{7,4},{8,9},{9,10},{10,1... | collective-permute-start | bytes 1966088 | tf_op jit(solution)/shard_map/ppermute | solution.py:25
  19.9 30.8 %collective-permute-start.2 = (bf16[1024,320]{0,1:T(8,128)(2,1)S(1)}, bf16[1024,320]{0,1:T(8,128)(2,1)S(1)}, u32[]{:S(2)}, u32[]{:S(2)}) collective-permute-start(bf16[1024,320]{0,1:T(8,128)(2,1)S(1)} %fusion.96), channel_id=1, source_target_pairs={{0,3},{1,0},{2,1},{3,2},{4,7},{5,4},{6,5},{7,6},{8,11},{9,8},{10,9... | collective-permute-start | bytes 1966088 | tf_op jit(solution)/shard_map/ppermute | solution.py:27
  76.2 167.4 %all-gather.6.cloned.1.call-start = ((), (), s32[]{:S(2)}) async-start(), calls=%async_computation.10 | async-start | bytes 6553600 | tf_op jit(solution)/shard_map/all_gather | solution.py:55
  203.0 377.4 %all-gather.8.cloned.1.call-start = ((), (), s32[]{:S(2)}) async-start(), calls=%async_computation.11 | async-start | bytes 3276800 | tf_op jit(solution)/shard_map/all_gather | solution.py:42
  554.8 163.1 %reduce-scatter.12.cloned.1.call-start = ((), (), s32[]{:S(2)}) async-start(), calls=%async_computation.12 | async-start | bytes 6553600 | tf_op jit(solution)/shard_map/reduce_scatter | solution.py:50
  586.1 286.7 %reduce-scatter.18.cloned.1.call-start = ((), (), s32[]{:S(2)}) async-start(), calls=%async_computation.16 | async-start | bytes 26214400 | tf_op jit(solution)/shard_map/reduce_scatter | solution.py:46
  586.2 40.1 %collective-permute-start.6 = (bf16[1024,320]{0,1:T(8,128)(2,1)S(1)}, bf16[1024,320]{0,1:T(8,128)(2,1)S(1)}, u32[]{:S(2)}, u32[]{:S(2)}) collective-permute-start(bf16[1024,320]{0,1:T(8,128)(2,1)S(1)} %bitcast.279), channel_id=1, source_target_pairs={{0,1},{1,2},{2,3},{3,0},{4,5},{5,6},{6,7},{7,4},{8,9},{9,10},{10,1... | collective-permute-start | bytes 1966088 | tf_op jit(solution)/shard_map/ppermute | solution.py:25
  587.7 63.6 %collective-permute-start.8 = (bf16[1024,320]{0,1:T(8,128)(2,1)S(1)}, bf16[1024,320]{0,1:T(8,128)(2,1)S(1)}, u32[]{:S(2)}, u32[]{:S(2)}) collective-permute-start(bf16[1024,320]{0,1:T(8,128)(2,1)S(1)} %bitcast.280), channel_id=1, source_target_pairs={{0,3},{1,0},{2,1},{3,2},{4,7},{5,4},{6,5},{7,6},{8,11},{9,8},{10,9... | collective-permute-start | bytes 1966088 | tf_op jit(solution)/shard_map/ppermute | solution.py:27
  626.3 53.8 %collective-permute-start.7 = (bf16[1024,320]{0,1:T(8,128)(2,1)S(1)}, bf16[1024,320]{0,1:T(8,128)(2,1)S(1)}, u32[]{:S(2)}, u32[]{:S(2)}) collective-permute-start(bf16[1024,320]{0,1:T(8,128)(2,1)S(1)} %collective-permute-done.6), channel_id=1, source_target_pairs={{0,1},{1,2},{2,3},{3,0},{4,5},{5,6},{6,7},{7,4},{8,9},{9,10},{10,1... | collective-permute-start | bytes 1966088 | tf_op jit(solution)/shard_map/ppermute | solution.py:25
  700.1 328.6 %reduce-scatter.14.cloned.1.call-start = ((), (), s32[]{:S(2)}) async-start(), calls=%async_computation.13 | async-start | bytes 26214400 | tf_op jit(solution)/shard_map/reduce_scatter | solution.py:46
  729.0 31.2 %collective-permute-start.5 = (bf16[1024,320]{0,1:T(8,128)(2,1)S(1)}, bf16[1024,320]{0,1:T(8,128)(2,1)S(1)}, u32[]{:S(2)}, u32[]{:S(2)}) collective-permute-start(bf16[1024,320]{0,1:T(8,128)(2,1)S(1)} %add_convert_fusion.3), channel_id=1, source_target_pairs={{0,3},{1,0},{2,1},{3,2},{4,7},{5,4},{6,5},{7,6},{8,11},{9,8},{10,9... | collective-permute-start | bytes 1966088 | tf_op jit(solution)/shard_map/ppermute | solution.py:27
  788.6 325.6 %all-gather.12.cloned.1.call-start = ((), (), s32[]{:S(2)}) async-start(), calls=%async_computation.17 | async-start | bytes 13107200 | tf_op jit(solution)/shard_map/all_gather | solution.py:42
  1043.9 176.8 %reduce-scatter.20.cloned.1.call-start = ((), (), s32[]{:S(2)}) async-start(), calls=%async_computation.18 | async-start | bytes 6553600 | tf_op jit(solution)/shard_map/reduce_scatter | solution.py:50
  1126.8 215.6 %reduce-scatter.22.cloned.1.call-start = ((), (), s32[]{:S(2)}) async-start(), calls=%async_computation.19 | async-start | bytes 6553600 | tf_op jit(solution)/shard_map/reduce_scatter | solution.py:46
  1232.7 28.5 %collective-permute-start.9 = (bf16[1024,320]{0,1:T(8,128)(2,1)S(1)}, bf16[1024,320]{0,1:T(8,128)(2,1)S(1)}, u32[]{:S(2)}, u32[]{:S(2)}) collective-permute-start(bf16[1024,320]{0,1:T(8,128)(2,1)S(1)} %fusion.120), channel_id=1, source_target_pairs={{0,1},{1,2},{2,3},{3,0},{4,5},{5,6},{6,7},{7,4},{8,9},{9,10},{10,1... | collective-permute-start | bytes 1966088 | tf_op jit(solution)/shard_map/ppermute | solution.py:25
  1234.8 30.5 %collective-permute-start.11 = (bf16[1024,320]{0,1:T(8,128)(2,1)S(1)}, bf16[1024,320]{0,1:T(8,128)(2,1)S(1)}, u32[]{:S(2)}, u32[]{:S(2)}) collective-permute-start(bf16[1024,320]{0,1:T(8,128)(2,1)S(1)} %fusion.120), channel_id=1, source_target_pairs={{0,3},{1,0},{2,1},{3,2},{4,7},{5,4},{6,5},{7,6},{8,11},{9,8},{10,9... | collective-permute-start | bytes 1966088 | tf_op jit(solution)/shard_map/ppermute | solution.py:27
  1290.1 724.1 %reduce-scatter.24.cloned.1.call-start = ((), (), s32[]{:S(2)}) async-start(), calls=%async_computation.20 | async-start | bytes 13107200 | tf_op jit(solution)/shard_map/reduce_scatter | solution.py:46
  1928.7 157.3 %all-gather.10.cloned.1.call-start = ((), (), s32[]{:S(2)}) async-start(), calls=%async_computation.14 | async-start | bytes 13107200 | tf_op jit(solution)/shard_map/all_gather | solution.py:42
  1935.8 207.2 %all-gather.14.cloned.1.call-start = ((), (), s32[]{:S(2)}) async-start(), calls=%async_computation.21 | async-start | bytes 9830400 | tf_op jit(solution)/shard_map/all_gather | solution.py:42
  2017.7 207.2 %all-reduce.13.cloned.1.call-start = ((), (), s32[]{:S(2)}) async-start(), calls=%async_computation.24 | async-start | bytes 5242880 | tf_op jit(solution)/shard_map/psum | solution.py:302
  2149.8 171.1 %reduce-scatter.26.cloned.1.call-start = ((), (), s32[]{:S(2)}) async-start(), calls=%async_computation.22 | async-start | bytes 6553600 | tf_op jit(solution)/shard_map/reduce_scatter | solution.py:50
  2157.8 259.6 %reduce-scatter.16.cloned.1.call-start = ((), (), s32[]{:S(2)}) async-start(), calls=%async_computation.15 | async-start | bytes 6553600 | tf_op jit(solution)/shard_map/reduce_scatter | solution.py:50
  2171.7 375.2 %all-reduce.11.cloned.1.call-start = ((), (), s32[]{:S(2)}) async-start(), calls=%async_computation.23 | async-start | bytes 163840 | tf_op jit(solution)/shard_map/psum | solution.py:291
  (65 other events, 6693.8 us)
Sparse Core Ops, SparseCore 0:
  76.3 121.0 reduce-scatter.9
  203.1 40.4 all-gather.5
  554.9 25.5 all-gather.7
  586.2 131.5 reduce-scatter.11
  720.3 152.4 reduce-scatter.17
  875.4 153.1 reduce-scatter.13
  1044.0 70.1 all-gather.11
  1126.9 93.7 reduce-scatter.19
  1290.2 52.1 reduce-scatter.21
  1928.9 85.2 reduce-scatter.23
  2015.8 70.1 all-gather.9
  2087.6 55.3 all-gather.13
  2149.9 74.9 all-reduce.12
  2227.1 93.7 reduce-scatter.25
  2323.0 94.2 reduce-scatter.15
  2423.4 123.4 all-reduce.10
